TPU v7x, 32 devices: a whole 2x2x4 slice. The times are simulated.
32 devices in a mesh: section: 8 (over y, x, core), dp: 4 (over z).
Axes of the slice: x: 2, y: 2, z: 4, core: 2. Of those that a mesh axis runs over, the one named last changes fastest.
Arguments:
- inputs: bfloat16 [4, 8, 128, 4096], P('dp', 'section'), may hold values from -6 to 6
- key_rows: bfloat16 [4, 8, 24, 4096], P('dp', None, None, 'section'), may hold values from -32 to 32
- value_rows: bfloat16 [4, 8, 24, 4096], P('dp', None, None, 'section'), may hold values from -6 to 6
- query_gain: float32 [8, 4096], P('section'), may hold values from 0.1 to 1.9
- cotangent: bfloat16 [4, 8, 128, 4096], P('dp', 'section'), may hold values from -6 to 6
Outputs:
- key_grads: bfloat16 [4, 8, 24, 4096], P('dp', None, None, 'section')
- value_grads: bfloat16 [4, 8, 24, 4096], P('dp', None, None, 'section')
- gain_grads: float32 [8, 4096], P('section')
All inputs are finite; a program needn't handle non-finite values.
Results may differ from a plain program's by a relative error of at most 0.008.
Values may be sent and summed in bfloat16 or wider, within the bound.
A program may use at most 64 MiB of HBM per device.

v0:
```python
import jax
import jax.numpy as jnp
from jax import lax
from jax.sharding import PartitionSpec as P

HEAD = 64
TICKS = 3


def from_behind(x, axis, by):
    length = lax.axis_size(axis)
    return lax.ppermute(x, axis, [(i, (i + by) % length) for i in range(length)])


def product(form, left, right):
    return jnp.einsum(form, left, right, preferred_element_type=jnp.float32)


def attend_forward(states, gain_row, key_block, value_block):
    floats = states.astype(jnp.float32)
    inverse = lax.rsqrt(jnp.mean(floats * floats, axis=-1, keepdims=True) + 1e-06)
    queries = (floats * inverse * gain_row).astype(jnp.bfloat16)
    tok_rows, width = states.shape
    src_rows = key_block.shape[0]
    heads_count = width // HEAD
    query_heads = queries.reshape(tok_rows, heads_count, HEAD)
    key_heads = key_block.reshape(src_rows, heads_count, HEAD)
    value_heads = value_block.reshape(src_rows, heads_count, HEAD)
    scores = product("shd,thd->hst", key_heads, query_heads) * HEAD ** (-0.5)
    highest = jnp.max(scores, axis=1, keepdims=True)
    weights = jnp.exp(scores - highest)
    probs = weights / jnp.sum(weights, axis=1, keepdims=True)
    probs_low = probs.astype(jnp.bfloat16)
    mixed = product("hst,shd->thd", probs_low, value_heads).reshape(tok_rows, width)
    produced = (floats + mixed).astype(jnp.bfloat16)
    return (produced, (inverse, queries, probs, probs_low))


def attend_backward(states, gain_row, key_block, value_block, saved, incoming, needed):
    inverse, queries, probs, probs_low = saved
    tok_rows, width = states.shape
    src_rows = key_block.shape[0]
    heads_count = width // HEAD
    query_heads = queries.reshape(tok_rows, heads_count, HEAD)
    key_heads = key_block.reshape(src_rows, heads_count, HEAD)
    value_heads = value_block.reshape(src_rows, heads_count, HEAD)
    grad_heads = incoming.reshape(tok_rows, heads_count, HEAD)
    dprob = product("shd,thd->hst", value_heads, grad_heads)
    dscore = (
        probs * (dprob - jnp.sum(probs * dprob, axis=1, keepdims=True)) * HEAD ** (-0.5)
    ).astype(jnp.bfloat16)
    value_step = product("hst,thd->shd", probs_low, grad_heads).reshape(src_rows, width)
    key_step = product("hst,thd->shd", dscore, query_heads).reshape(src_rows, width)
    dquery = product("hst,shd->thd", dscore, key_heads).reshape(tok_rows, width)
    unit = states.astype(jnp.float32) * inverse
    gain_step = jnp.sum(dquery * unit, axis=0)
    if needed:
        scaled = gain_row * dquery
        back = incoming.astype(jnp.float32) + inverse * (
            scaled - unit * jnp.mean(scaled * unit, axis=-1, keepdims=True)
        )
        back = back.astype(jnp.bfloat16)
    else:
        back = None
    return (back, key_step, value_step, gain_step)


def on_device(inputs, key_rows, value_rows, query_gain, cotangent):
    arrived = (
        lax.all_to_all(key_rows, "section", split_axis=1, concat_axis=3, tiled=True),
        lax.all_to_all(value_rows, "section", split_axis=1, concat_axis=3, tiled=True),
    )
    local_keys = arrived[0][0, 0]
    local_values = arrived[1][0, 0]
    gain_row = query_gain[0]
    current = inputs[0, 0]
    states = [current]
    for tick_index in range(TICKS):
        if tick_index + 1 < TICKS:
            produced, saved = attend_forward(current, gain_row, local_keys, local_values)
        if tick_index + 1 < TICKS:
            current = from_behind(produced, "section", 1)
            states.append(current)
    key_total = jnp.zeros(local_keys.shape, jnp.float32)
    value_total = jnp.zeros(local_values.shape, jnp.float32)
    gain_total = jnp.zeros(gain_row.shape, jnp.float32)
    carried = cotangent[0, 0]
    for tick_index in range(TICKS - 1, -1, -1):
        incoming = from_behind(carried, "section", -1)
        saved = attend_forward(states[tick_index], gain_row, local_keys, local_values)[1]
        carried, key_step, value_step, gain_step = attend_backward(
            states[tick_index], gain_row, local_keys, local_values, saved, incoming, tick_index > 0
        )
        key_total = key_total + key_step
        value_total = value_total + value_step
        gain_total = gain_total + gain_step
    returned = (
        lax.all_to_all(
            key_total.astype(jnp.bfloat16)[None, None],
            "section",
            split_axis=3,
            concat_axis=1,
            tiled=True,
        ),
        lax.all_to_all(
            value_total.astype(jnp.bfloat16)[None, None],
            "section",
            split_axis=3,
            concat_axis=1,
            tiled=True,
        ),
    )
    gain_summed = lax.psum(gain_total, "dp")
    return (returned[0], returned[1], gain_summed[None])


def solution(mesh):
    return jax.shard_map(
        on_device,
        mesh=mesh,
        in_specs=(
            P("dp", "section", None, None),
            P("dp", None, None, "section"),
            P("dp", None, None, "section"),
            P("section", None),
            P("dp", "section", None, None),
        ),
        out_specs=(
            P("dp", None, None, "section"),
            P("dp", None, None, "section"),
            P("section", None),
        ),
        check_vma=False,
    )
```

profile of v0, /device:TPU:0, one launch (start us, length us, event | category | flops | bytes accessed | tf_op | source)
XLA Modules:
  0.0 241.4 jit_solution(5786657829530134387)
XLA Ops:
  0.6 5.2 %all-to-all-start = ((bf16[1,8,24,512]{3,2,0,1:T(8,128)(2,1)}), bf16[1,8,24,512]{3,2,0,1:T(8,128)(2,1)S(1)}, u32[]{:S(2)}, u32[]{:S(2)}) async-start(bf16[1,8,24,512]{3,2,0,1:T(8,128)(2,1)} %bitcast.148), calls=%async_computation | async-start | bytes 393216 | tf_op jit(solution)/shard_map/all_to_all | solution.py:70
  5.8 0.5 broadcast.121
  6.4 1.4 reduce.4
  7.8 1.6 copy.41
  9.5 0.6 fusion.33
  10.0 2.0 all-to-all-done
  12.0 3.4 %all-to-all-start.1 = ((bf16[1,8,24,512]{3,2,0,1:T(8,128)(2,1)}), bf16[1,8,24,512]{3,2,0,1:T(8,128)(2,1)S(1)}, u32[]{:S(2)}, u32[]{:S(2)}) async-start(bf16[1,8,24,512]{3,2,0,1:T(8,128)(2,1)} %bitcast.6), calls=%async_computation.1 | async-start | bytes 393216 | tf_op jit(solution)/shard_map/all_to_all | solution.py:71
  15.5 6.0 %all-to-all-done.1 = bf16[1,8,24,512]{3,2,0,1:T(8,128)(2,1)S(1)} async-done(((bf16[1,8,24,512]{3,2,0,1:T(8,128)(2,1)}), bf16[1,8,24,512]{3,2,0,1:T(8,128)(2,1)S(1)}, u32[]{:S(2)}, u32[]{:S(2)}) %all-to-all-start.1) | async-done | bytes 196640 | tf_op jit(solution)/shard_map/all_to_all | solution.py:71
  22.1 0.7 fusion.54
  22.9 1.8 fusion.114
  24.6 2.0 fusion.90
  26.7 1.2 fusion.31
  27.9 2.3 copy.51
  30.2 2.6 %collective-permute-start.2 = (bf16[128,4096]{0,1:T(8,128)(2,1)}, bf16[128,4096]{0,1:T(8,128)(2,1)}, u32[]{:S(2)}, u32[]{:S(2)}) collective-permute-start(bf16[128,4096]{0,1:T(8,128)(2,1)} %bitcast.18), channel_id=1, source_target_pairs={{0,28},{4,0},{8,4},{12,8},{16,12},{20,16},{24,20},{28,24},{1,29},{... | collective-permute-start | bytes 3145736 | tf_op jit(solution)/shard_map/ppermute | solution.py:12
  32.8 19.4 %collective-permute-done = bf16[128,4096]{0,1:T(8,128)(2,1)S(1)} collective-permute-done((bf16[128,4096]{0,1:T(8,128)(2,1)}, bf16[128,4096]{0,1:T(8,128)(2,1)S(1)}, u32[]{:S(2)}, u32[]{:S(2)}) %collective-permute-start) | collective-permute-done | bytes 1048608 | tf_op jit(solution)/shard_map/ppermute | solution.py:12
  52.2 0.6 fusion.29
  52.8 0.7 fusion.22
  53.5 0.4 fusion.53
  54.0 0.9 copy-done.11
  54.9 1.7 fusion.115
  56.5 3.3 %fusion.88 = f32[64,128,64]{1,2,0:T(8,128)} fusion(bf16[24,64,64]{2,1,0:T(8,128)(2,1)S(1)} %reshape_squeeze.5, f32[64,128]{1,0:T(8,128)} %get-tuple-element.15, f32[64,24,128]{2,1,0:T(8,128)} %copy-done.11), kind=kOutput, calls=%fused_computation.108 | convolution fusion | flops 25763864 | bytes 3112960 | tf_op jit(solution)/shard_map/hst,shd->thd/dot_general | solution.py:16
  59.9 1.8 fusion.30
  61.8 2.6 %fusion.86 = f32[64,24,128]{2,1,0:T(8,128)} fusion(bf16[128,64,64]{0,2,1:T(8,128)(2,1)} %bitcast.19, bf16[24,64,64]{2,1,0:T(8,128)(2,1)S(1)} %reshape_squeeze.5), kind=kOutput, calls=%fused_computation.106 | convolution fusion | flops 25165824 | bytes 2031616 | tf_op jit(solution)/shard_map/shd,thd->hst/dot_general | solution.py:16
  64.4 12.5 %collective-permute-done.1 = bf16[128,4096]{0,1:T(8,128)(2,1)S(1)} collective-permute-done((bf16[128,4096]{0,1:T(8,128)(2,1)S(1)}, bf16[128,4096]{0,1:T(8,128)(2,1)S(1)}, u32[]{:S(2)}, u32[]{:S(2)}) %collective-permute-start.1) | collective-permute-done | bytes 1048608 | tf_op jit(solution)/shard_map/ppermute | solution.py:12
  76.9 0.6 fusion.21
  77.4 0.7 fusion.14
  78.2 1.0 copy-done.2
  79.1 0.4 fusion.52
  79.6 0.9 copy-done.10
  80.5 1.7 fusion.116
  82.2 4.0 %fusion.61 = f32[64,128,64]{1,2,0:T(8,128)} fusion(f32[64,24,128]{2,1,0:T(8,128)} %fusion.86, bf16[24,64,64]{2,1,0:T(8,128)(2,1)} %copy-done.6, f32[64,24,128]{2,1,0:T(8,128)} %get-tuple-element.18, f32[64,128]{1,0:T(8,128)} %get-tuple-element.17), kind=kOutput, calls=%fused_computation.81 | convolution fusion | flops 26550296 | bytes 3899392 | tf_op jit(solution)/shard_map/hst,shd->thd/dot_general | solution.py:16
  86.2 3.3 %fusion.20 = (f32[4096]{0:T(1024)}, f32[128]{0:T(128)S(1)}) fusion(bf16[128,4096]{0,1:T(8,128)(2,1)S(1)} %collective-permute-done.1, f32[64,128,64]{1,2,0:T(8,128)} %fusion.61, f32[128]{0:T(128)} %copy-done.23, f32[4096]{0:T(1024)S(1)} %bitcast.138), kind=kLoop, calls=%fused_computation.25 | loop fusion | flops 3665792 | bytes 3179520 | tf_op jit(solution)/shard_map/reduce_sum | solution.py:56
  89.5 1.9 fusion.19
  91.5 12.3 %collective-permute-done.3 = bf16[128,4096]{0,1:T(8,128)(2,1)S(1)} collective-permute-done((bf16[128,4096]{0,1:T(8,128)(2,1)S(1)}, bf16[128,4096]{0,1:T(8,128)(2,1)S(1)}, u32[]{:S(2)}, u32[]{:S(2)}) %collective-permute-start.3) | collective-permute-done | bytes 1048608 | tf_op jit(solution)/shard_map/ppermute | solution.py:12
  103.8 1.3 convolution_bitcast_fusion.4
  105.1 4.0 %fusion.66 = f32[64,128,64]{1,2,0:T(8,128)} fusion(f32[64,24,128]{2,1,0:T(8,128)} %convolution_bitcast_fusion.4, bf16[24,64,64]{2,1,0:T(8,128)(2,1)} %copy-done.6, f32[64,24,128]{2,1,0:T(8,128)} %get-tuple-element.16, f32[64,128]{1,0:T(8,128)} %get-tuple-element.15), kind=kOutput, calls=%fused_computation.85 | convolution fusion | flops 26550296 | bytes 3899392 | tf_op jit(solution)/shard_map/hst,shd->thd/dot_general | solution.py:16
  109.1 3.3 %fusion.28 = (f32[4096]{0:T(1024)}, f32[128]{0:T(128)S(1)}) fusion(bf16[128,4096]{0,1:T(8,128)(2,1)S(1)} %collective-permute-done, f32[64,128,64]{1,2,0:T(8,128)} %fusion.66, f32[128]{0:T(128)} %copy-done.21, f32[4096]{0:T(1024)S(1)} %bitcast.140), kind=kLoop, calls=%fused_computation.33 | loop fusion | flops 3665792 | bytes 3179520 | tf_op jit(solution)/shard_map/reduce_sum | solution.py:56
  112.3 1.8 fusion.27
  114.2 2.8 %collective-permute-start.4 = (bf16[128,4096]{0,1:T(8,128)(2,1)}, bf16[128,4096]{0,1:T(8,128)(2,1)}, u32[]{:S(2)}, u32[]{:S(2)}) collective-permute-start(bf16[128,4096]{0,1:T(8,128)(2,1)} %fusion.27), channel_id=1, source_target_pairs={{0,28},{4,0},{8,4},{12,8},{16,12},{20,16},{24,20},{28,24},{1,29},{... | collective-permute-start | bytes 3145736 | tf_op jit(solution)/shard_map/ppermute | solution.py:12
  117.0 3.0 %convolution_bitcast_fusion.1 = f32[24,64,64]{2,0,1:T(8,128)} fusion(bf16[128,64,64]{0,2,1:T(8,128)(2,1)S(1)} %bitcast.135, f32[64,128]{1,0:T(8,128)} %get-tuple-element.15, f32[64,24,128]{2,1,0:T(8,128)} %copy-done.11), kind=kOutput, calls=%fused_computation.52 | convolution fusion | flops 25763864 | bytes 2260992 | tf_op jit(solution)/shard_map/hst,thd->shd/dot_general | solution.py:16
  119.9 3.4 %fusion.67 = f32[64,64,24]{1,2,0:T(8,128)} fusion(bf16[128,64,64]{0,2,1:T(8,128)(2,1)S(1)} %bitcast.133, f32[64,24,128]{2,1,0:T(8,128)} %convolution_bitcast_fusion.4, f32[64,24,128]{2,1,0:T(8,128)} %get-tuple-element.16, f32[64,128]{1,0:T(8,128)} %get-tuple-element.15), kind=kOutput, calls=%fused_computation.86 | convolution fusion | flops 26550296 | bytes 3047424 | tf_op jit(solution)/shard_map/hst,thd->shd/dot_general | solution.py:16
  123.3 6.2 %collective-permute-done.4 = bf16[128,4096]{0,1:T(8,128)(2,1)} collective-permute-done((bf16[128,4096]{0,1:T(8,128)(2,1)}, bf16[128,4096]{0,1:T(8,128)(2,1)}, u32[]{:S(2)}, u32[]{:S(2)}) %collective-permute-start.4) | collective-permute-done | bytes 1048608 | tf_op jit(solution)/shard_map/ppermute | solution.py:12
  129.6 3.3 %convolution_bitcast_fusion = f32[24,64,64]{2,0,1:T(8,128)} fusion(bf16[128,64,64]{0,2,1:T(8,128)(2,1)} %bitcast.26, f32[64,128]{1,0:T(8,128)S(1)} %copy-done.17, f32[64,24,128]{2,1,0:T(8,128)} %copy-done.14), kind=kOutput, calls=%fused_computation.51 | convolution fusion | flops 25763864 | bytes 2260992 | tf_op jit(solution)/shard_map/hst,thd->shd/dot_general | solution.py:16
  132.9 1.7 convolution_bitcast_fusion.3
  134.7 1.2 fusion.32
  135.9 1.6 fusion.72
  137.6 2.9 %fusion.59 = bf16[24,64,64]{2,0,1:T(8,128)(2,1)S(1)} fusion(f32[24,64,64]{2,0,1:T(8,128)} %convolution_bitcast_fusion, f32[24,64,64]{2,0,1:T(8,128)} %convolution_bitcast_fusion.1, bf16[128,64,64]{0,2,1:T(8,128)(2,1)} %bitcast.19, f32[64,128]{1,0:T(8,128)S(1)} %copy-done.18, f32[64,24,128]{2,1,0:T(8,128)} %copy-done.10), kind=kOutput, calls=%fused_computation.79 | convolution fusion | flops 26058776 | bytes 2850816 | tf_op jit(solution)/shard_map/hst,thd->shd/dot_general | solution.py:16
  140.9 2.8 %copy.61 = bf16[1,1,24,4096]{2,1,0,3:T(2,128)(2,1)S(1)} copy(bf16[1,1,24,4096]{3,2,1,0:T(8,128)(2,1)S(1)} %convert_element_type.128) | data formatting | bytes 393216 | tf_op jit(solution)/shard_map/convert_element_type | solution.py:106
  143.7 0.5 broadcast.122
  144.2 23.5 %reduce.6 = bf16[4096,24]{1,0:T(8,128)(2,1)} reduce(bf16[4096,1,1,24]{3,2,1,0:T(2,128)(2,1)S(1)} %bitcast.126, bf16[]{:T(256)} %broadcast.122), dimensions={1,2}, to_apply=%bitcast.103.reduce_sub_computation | reduce | bytes 393218
  167.7 3.4 %reshape.199 = bf16[8,2,6144]{2,1,0:T(2,128)(2,1)} reshape(bf16[4096,24]{1,0:T(8,128)(2,1)} %reduce.6) | data formatting | bytes 393216
  171.0 4.1 %all-to-all-start.3 = ((bf16[8,2,6144]{2,1,0:T(2,128)(2,1)}), bf16[8,2,6144]{2,1,0:T(2,128)(2,1)S(1)}, u32[]{:S(2)}, u32[]{:S(2)}) async-start(bf16[8,2,6144]{2,1,0:T(2,128)(2,1)} %reshape.199), calls=%async_computation.3 | async-start | bytes 393216 | tf_op jit(solution)/shard_map/all_to_all | solution.py:105
  175.1 3.0 %fusion.60 = bf16[24,64,64]{2,0,1:T(8,128)(2,1)S(1)} fusion(f32[64,64,24]{1,2,0:T(8,128)} %fusion.72, f32[64,64,24]{1,2,0:T(8,128)} %fusion.67, bf16[128,64,64]{0,2,1:T(8,128)(2,1)S(1)} %bitcast.131, f32[64,24,128]{2,1,0:T(8,128)} %fusion.86, f32[64,24,128]{2,1,0:T(8,128)} %get-tuple-element.18, f32[64,128]{1,0:T(8,128)S(1)} %copy-done.18), kind=kOutput, calls=%fused_computation.80 | convolution fusion | flops 26845208 | bytes 3637248 | tf_op jit(solution)/shard_map/hst,thd->shd/dot_general | solution.py:16
  178.6 2.8 %copy.58 = bf16[1,1,24,4096]{2,1,0,3:T(2,128)(2,1)S(1)} copy(bf16[1,1,24,4096]{3,2,1,0:T(8,128)(2,1)S(1)} %convert_element_type.125) | data formatting | bytes 393216 | tf_op jit(solution)/shard_map/convert_element_type | solution.py:99
  181.4 22.4 %reduce.5 = bf16[4096,24]{1,0:T(8,128)(2,1)S(1)} reduce(bf16[4096,1,1,24]{3,2,1,0:T(2,128)(2,1)S(1)} %bitcast.127, bf16[]{:T(256)} %broadcast.122), dimensions={1,2}, to_apply=%bitcast.101.reduce_sub_computation | reduce | bytes 393218
  203.8 2.0 reshape.197
  205.8 4.2 %all-to-all-start.2 = ((bf16[8,2,6144]{2,1,0:T(2,128)(2,1)}), bf16[8,2,6144]{2,1,0:T(2,128)(2,1)S(1)}, u32[]{:S(2)}, u32[]{:S(2)}) async-start(bf16[8,2,6144]{2,1,0:T(2,128)(2,1)} %reshape.197), calls=%async_computation.2 | async-start | bytes 393216 | tf_op jit(solution)/shard_map/all_to_all | solution.py:98
  210.0 19.6 %psum.7 = f32[1,4096]{1,0:T(1,128)} all-reduce(f32[1,4096]{1,0:T(1,128)S(1)} %bitcast.149), channel_id=1, replica_groups=mesh['section'=8,'dp'=4] {'dp'}, use_global_device_ids=true, to_apply=%region_17.0 | all-reduce | flops 4096 | bytes 32768 | tf_op jit(solution)/shard_map/psum | solution.py:113
  229.6 3.0 %reshape.200 = bf16[4096,1,1,24]{3,2,1,0:T(2,128)(2,1)S(1)} reshape(bf16[8,2,6144]{2,1,0:T(2,128)(2,1)S(1)} %all-to-all-done.3) | data formatting | bytes 393216
  232.6 2.1 copy.62
  234.8 0.7 copy.65
  235.5 3.0 %reshape.198 = bf16[4096,1,1,24]{3,2,1,0:T(2,128)(2,1)S(1)} reshape(bf16[8,2,6144]{2,1,0:T(2,128)(2,1)S(1)} %all-to-all-done.2) | data formatting | bytes 393216
  238.5 2.1 copy.59
  240.7 0.7 copy.64
  (75 shorter events, 2.0 us)
Async XLA Ops:
  0.6 11.4 %all-to-all-start = ((bf16[1,8,24,512]{3,2,0,1:T(8,128)(2,1)}), bf16[1,8,24,512]{3,2,0,1:T(8,128)(2,1)S(1)}, u32[]{:S(2)}, u32[]{:S(2)}) async-start(bf16[1,8,24,512]{3,2,0,1:T(8,128)(2,1)} %bitcast.148), calls=%async_computation | async-start | bytes 393216 | tf_op jit(solution)/shard_map/all_to_all | solution.py:70
  7.8 14.3 %copy-start.19 = (f32[64,64]{1,0:T(8,128)}, f32[64,64]{1,0:T(8,128)S(1)}, u32[]{:S(2)}) copy-start(f32[64,64]{1,0:T(8,128)S(1)} %mul.98) | copy-start | bytes 49156
  12.0 9.5 %all-to-all-start.1 = ((bf16[1,8,24,512]{3,2,0,1:T(8,128)(2,1)}), bf16[1,8,24,512]{3,2,0,1:T(8,128)(2,1)S(1)}, u32[]{:S(2)}, u32[]{:S(2)}) async-start(bf16[1,8,24,512]{3,2,0,1:T(8,128)(2,1)} %bitcast.6), calls=%async_computation.1 | async-start | bytes 393216 | tf_op jit(solution)/shard_map/all_to_all | solution.py:71
  15.5 7.4 %copy-start.25 = (f32[128]{0:T(128)}, f32[128]{0:T(128)S(1)}, u32[]{:S(2)}) copy-start(f32[128]{0:T(128)S(1)} %add_rsqrt_fusion.2) | copy-start | bytes 1540
  21.9 2.7 %copy-start.6 = (bf16[24,64,64]{2,1,0:T(8,128)(2,1)}, bf16[24,64,64]{2,1,0:T(8,128)(2,1)S(1)}, u32[]{:S(2)}) copy-start(bf16[24,64,64]{2,1,0:T(8,128)(2,1)S(1)} %reshape_squeeze.4) | copy-start | bytes 589828
  22.9 1.8 copy-start.14
  27.9 24.9 %copy-start.12 = (f32[1,4096]{1,0:T(1,128)S(1)}, f32[1,4096]{1,0:T(1,128)}, u32[]{:S(2)}) copy-start(f32[1,4096]{1,0:T(1,128)} %param.8) | copy-start | bytes 49156
  27.9 24.3 %collective-permute-start = (bf16[128,4096]{0,1:T(8,128)(2,1)}, bf16[128,4096]{0,1:T(8,128)(2,1)S(1)}, u32[]{:S(2)}, u32[]{:S(2)}) collective-permute-start(bf16[128,4096]{0,1:T(8,128)(2,1)} %fusion.31), channel_id=1, source_target_pairs={{0,4},{4,8},{8,12},{12,16},{16,20},{20,24},{24,28},{28,0},{1,5},{5... | collective-permute-start | bytes 3145736 | tf_op jit(solution)/shard_map/ppermute | solution.py:12
  30.2 23.4 %copy-start.7 = (bf16[24,64,64]{2,1,0:T(8,128)(2,1)S(1)}, bf16[24,64,64]{2,1,0:T(8,128)(2,1)}, u32[]{:S(2)}) copy-start(bf16[24,64,64]{2,1,0:T(8,128)(2,1)} %copy-done.6) | copy-start | bytes 589828
  30.2 31.6 %collective-permute-start.2 = (bf16[128,4096]{0,1:T(8,128)(2,1)}, bf16[128,4096]{0,1:T(8,128)(2,1)}, u32[]{:S(2)}, u32[]{:S(2)}) collective-permute-start(bf16[128,4096]{0,1:T(8,128)(2,1)} %bitcast.18), channel_id=1, source_target_pairs={{0,28},{4,0},{8,4},{12,8},{16,12},{20,16},{24,20},{28,24},{1,29},{... | collective-permute-start | bytes 3145736 | tf_op jit(solution)/shard_map/ppermute | solution.py:12
  52.8 0.7 copy-start.21
  53.5 6.4 %copy-start.4 = (bf16[128,4096]{0,1:T(8,128)(2,1)}, bf16[128,4096]{0,1:T(8,128)(2,1)S(1)}, u32[]{:S(2)}) copy-start(bf16[128,4096]{0,1:T(8,128)(2,1)S(1)} %fusion.22) | copy-start | bytes 3145732
  54.0 0.9 copy-start.11
  61.7 15.2 %collective-permute-start.1 = (bf16[128,4096]{0,1:T(8,128)(2,1)S(1)}, bf16[128,4096]{0,1:T(8,128)(2,1)S(1)}, u32[]{:S(2)}, u32[]{:S(2)}) collective-permute-start(bf16[128,4096]{0,1:T(8,128)(2,1)S(1)} %fusion.30), channel_id=1, source_target_pairs={{0,4},{4,8},{8,12},{12,16},{16,20},{20,24},{24,28},{28,0},{1,5},{5... | collective-permute-start | bytes 3145736 | tf_op jit(solution)/shard_map/ppermute | solution.py:12
  64.4 14.8 %copy-start.8 = (bf16[24,64,64]{2,1,0:T(8,128)(2,1)S(1)}, bf16[24,64,64]{2,1,0:T(8,128)(2,1)}, u32[]{:S(2)}) copy-start(bf16[24,64,64]{2,1,0:T(8,128)(2,1)} %copy-done.6) | copy-start | bytes 589828
  77.4 0.7 copy-start.23
  78.2 1.0 copy-start.2
  79.6 0.9 copy-start.10
  86.2 3.3 %copy-start = (f32[64,128,64]{1,2,0:T(8,128)S(1)}, f32[64,128,64]{1,2,0:T(8,128)}, u32[]{:S(2)}) copy-start(f32[64,128,64]{1,2,0:T(8,128)} %fusion.61) | copy-start | bytes 6291460
  86.2 3.3 %copy-start.24 = (f32[128]{0:T(128)S(1)}, f32[128]{0:T(128)}, u32[]{:S(2)}) copy-start(f32[128]{0:T(128)} %copy-done.23) | copy-start | bytes 1540
  91.4 12.4 %collective-permute-start.3 = (bf16[128,4096]{0,1:T(8,128)(2,1)S(1)}, bf16[128,4096]{0,1:T(8,128)(2,1)S(1)}, u32[]{:S(2)}, u32[]{:S(2)}) collective-permute-start(bf16[128,4096]{0,1:T(8,128)(2,1)S(1)} %fusion.19), channel_id=1, source_target_pairs={{0,28},{4,0},{8,4},{12,8},{16,12},{20,16},{24,20},{28,24},{1,29},{... | collective-permute-start | bytes 3145736 | tf_op jit(solution)/shard_map/ppermute | solution.py:12
  109.1 3.3 %copy-start.1 = (f32[64,128,64]{1,2,0:T(8,128)S(1)}, f32[64,128,64]{1,2,0:T(8,128)}, u32[]{:S(2)}) copy-start(f32[64,128,64]{1,2,0:T(8,128)} %fusion.66) | copy-start | bytes 6291460
  109.1 3.3 %copy-start.22 = (f32[128]{0:T(128)S(1)}, f32[128]{0:T(128)}, u32[]{:S(2)}) copy-start(f32[128]{0:T(128)} %copy-done.21) | copy-start | bytes 1540
  114.2 5.8 %copy-start.5 = (bf16[128,4096]{0,1:T(8,128)(2,1)S(1)}, bf16[128,4096]{0,1:T(8,128)(2,1)}, u32[]{:S(2)}) copy-start(bf16[128,4096]{0,1:T(8,128)(2,1)} %copy-done.4) | copy-start | bytes 3145732
  114.2 15.4 %collective-permute-start.4 = (bf16[128,4096]{0,1:T(8,128)(2,1)}, bf16[128,4096]{0,1:T(8,128)(2,1)}, u32[]{:S(2)}, u32[]{:S(2)}) collective-permute-start(bf16[128,4096]{0,1:T(8,128)(2,1)} %fusion.27), channel_id=1, source_target_pairs={{0,28},{4,0},{8,4},{12,8},{16,12},{20,16},{24,20},{28,24},{1,29},{... | collective-permute-start | bytes 3145736 | tf_op jit(solution)/shard_map/ppermute | solution.py:12
  119.9 9.7 %copy-start.17 = (f32[64,128]{1,0:T(8,128)S(1)}, f32[64,128]{1,0:T(8,128)}, u32[]{:S(2)}) copy-start(f32[64,128]{1,0:T(8,128)} %get-tuple-element.13) | copy-start | bytes 98308
  132.9 1.8 copy-start.9
  132.9 1.8 copy-start.13
  132.9 1.8 copy-start.26
  134.7 1.2 copy-start.20
  135.8 1.7 copy-start.18
  144.2 30.9 %copy-start.3 = (bf16[128,4096]{0,1:T(8,128)(2,1)S(1)}, bf16[128,4096]{0,1:T(8,128)(2,1)}, u32[]{:S(2)}) copy-start(bf16[128,4096]{0,1:T(8,128)(2,1)} %copy-done.2) | copy-start | bytes 3145732
  171.0 34.8 %all-to-all-start.3 = ((bf16[8,2,6144]{2,1,0:T(2,128)(2,1)}), bf16[8,2,6144]{2,1,0:T(2,128)(2,1)S(1)}, u32[]{:S(2)}, u32[]{:S(2)}) async-start(bf16[8,2,6144]{2,1,0:T(2,128)(2,1)} %reshape.199), calls=%async_computation.3 | async-start | bytes 393216 | tf_op jit(solution)/shard_map/all_to_all | solution.py:105
  181.3 28.7 %copy-start.15 = (f32[4096]{0:T(1024)S(1)}, f32[4096]{0:T(1024)}, u32[]{:S(2)}) copy-start(f32[4096]{0:T(1024)} %get-tuple-element.11) | copy-start | bytes 49156
  181.4 28.6 %copy-start.16 = (f32[4096]{0:T(1024)S(1)}, f32[4096]{0:T(1024)}, u32[]{:S(2)}) copy-start(f32[4096]{0:T(1024)} %get-tuple-element.9) | copy-start | bytes 49156
  205.8 29.7 %all-to-all-start.2 = ((bf16[8,2,6144]{2,1,0:T(2,128)(2,1)}), bf16[8,2,6144]{2,1,0:T(2,128)(2,1)S(1)}, u32[]{:S(2)}, u32[]{:S(2)}) async-start(bf16[8,2,6144]{2,1,0:T(2,128)(2,1)} %reshape.197), calls=%async_computation.2 | async-start | bytes 393216 | tf_op jit(solution)/shard_map/all_to_all | solution.py:98
where the time goes:
time: 242 us; the launch traced here: 241 us
  other arithmetic  68.8 us (28%)
  waiting for transfers between devices  58.5 us (24%)
  matrix products  39 us (16%)
  local copies, waits for them, and re-layouts  32 us (13%)
  starting transfers between devices  22.4 us (9%)
  blocking collectives  19.6 us (8%)
    ppermute x5, waiting for transfers between devices, from_behind(): lax.ppermute(x, axis, [(i, (i + by) % length) for i in range(length)])  50.5 us
    unnamed x3, other arithmetic  47.3 us
    dot_general x17, matrix products, product(): return jnp.einsum(form, left, right, preferred_element_type=jnp.float32)  39 us
    unnamed x66, local copies, waits for them, and re-layouts  20.7 us
    psum x1, blocking collectives, on_device(): gain_summed = lax.psum(gain_total, 'dp')  19.6 us
    reduce_sum x2, other arithmetic, attend_backward(): gain_step = jnp.sum(dquery * unit, axis=0)  6.51 us
    all_to_all x1, waiting for transfers between devices, on_device(): lax.all_to_all(value_rows, 'section', split_axis=1, concat_axis=3, tiled=...  6.05 us
    ppermute x5, starting transfers between devices, from_behind(): lax.ppermute(x, axis, [(i, (i + by) % length) for i in range(length)])  5.55 us
  transfers between devices with their start and end apart: 9, of which 6 were waited for; matrix products, arithmetic and copies ran while one was open for 25% of the time, Pallas kernels for 0%

commit v1 on v0

--- a/solution.py
+++ b/solution.py
@@ -67,7 +67,12 @@
 
 def on_device(inputs, key_rows, value_rows, query_gain, cotangent):
     arrived = (
-        lax.all_to_all(key_rows, "section", split_axis=1, concat_axis=3, tiled=True),
+        jnp.concatenate(
+            lax.all_to_all(
+                jnp.stack(jnp.split(key_rows, lax.axis_size("section"), axis=1)), "section", 0, 0
+            ),
+            axis=3,
+        ),
         lax.all_to_all(value_rows, "section", split_axis=1, concat_axis=3, tiled=True),
     )
     local_keys = arrived[0][0, 0]

time: 242 us -> 256 us (1.058)
  local copies, waits for them, and re-layouts: 32 us -> 42.7 us
    unnamed x66 -> x77, local copies, waits for them, and re-layouts: 20.7 us -> 29.8 us
    all_to_all x1, waiting for transfers between devices: 6.05 us -> 0.01 us  [on_device(): lax.all_to_all(value_rows, 'section', split_axis=1, concat_axis=3, tiled=...]
    all_to_all x1, waiting for transfers between devices: 2.02 us -> 5.89 us  [on_device(): lax.all_to_all(jnp.stack(jnp.split(key_rows, lax.axis_size('section'), ax...]
  transfers between devices with their start and end apart: 9 -> 9, of which waited for: 6 -> 5; matrix products, arithmetic and copies ran while one was open for 25% -> 28% of each run, Pallas kernels for 0% -> 0%
where the time goes in v1:
time: 256 us; the launch traced here: 254 us
  other arithmetic  69.9 us (27%)
  waiting for transfers between devices  58.2 us (23%)
  local copies, waits for them, and re-layouts  42.7 us (17%)
  matrix products  39.2 us (15%)
  starting transfers between devices  23.4 us (9%)
  blocking collectives  19.6 us (8%)
    ppermute x5, waiting for transfers between devices, from_behind(): lax.ppermute(x, axis, [(i, (i + by) % length) for i in range(length)])  52.4 us
    unnamed x3, other arithmetic  47.3 us
    dot_general x17, matrix products, product(): return jnp.einsum(form, left, right, preferred_element_type=jnp.float32)  39.2 us
    unnamed x77, local copies, waits for them, and re-layouts  29.8 us
    psum x1, blocking collectives, on_device(): gain_summed = lax.psum(gain_total, 'dp')  19.6 us
    reduce_sum x2, other arithmetic, attend_backward(): gain_step = jnp.sum(dquery * unit, axis=0)  6.51 us
    all_to_all x1, waiting for transfers between devices, on_device(): lax.all_to_all(jnp.stack(jnp.split(key_rows, lax.axis_size('section'), ax...  5.89 us
    ppermute x5, starting transfers between devices, from_behind(): lax.ppermute(x, axis, [(i, (i + by) % length) for i in range(length)])  5.73 us
  transfers between devices with their start and end apart: 9, of which 5 were waited for; matrix products, arithmetic and copies ran while one was open for 28% of the time, Pallas kernels for 0%

profile of v1, /device:TPU:0, one launch (start us, length us, event | category | flops | bytes accessed | tf_op | source)
XLA Modules:
  0.0 254.1 jit_solution(8776048380150414373)
XLA Ops:
  0.6 5.2 %all-to-all-start.1 = ((bf16[1,8,24,512]{3,2,0,1:T(8,128)(2,1)}), bf16[1,8,24,512]{3,2,0,1:T(8,128)(2,1)S(1)}, u32[]{:S(2)}, u32[]{:S(2)}) async-start(bf16[1,8,24,512]{3,2,0,1:T(8,128)(2,1)} %bitcast.156), calls=%async_computation.1 | async-start | bytes 393216 | tf_op jit(solution)/shard_map/all_to_all | solution.py:76
  6.4 1.4 reduce.4
  7.8 1.4 bitcast_dynamic-update-slice_fusion.7
  9.2 1.3 bitcast_dynamic-update-slice_fusion.6
  10.5 1.3 bitcast_dynamic-update-slice_fusion.5
  11.9 1.3 bitcast_dynamic-update-slice_fusion.4
  13.2 1.3 bitcast_dynamic-update-slice_fusion.3
  14.6 1.3 bitcast_dynamic-update-slice_fusion.2
  15.9 1.3 bitcast_dynamic-update-slice_fusion.1
  17.3 1.3 bitcast_dynamic-update-slice_fusion
  18.6 1.6 copy.41
  20.8 4.2 %all-to-all-start = ((bf16[8,1,1,24,512]{4,3,2,1,0:T(8,128)(2,1)}), bf16[8,1,1,24,512]{4,3,2,1,0:T(8,128)(2,1)S(1)}, u32[]{:S(2)}, u32[]{:S(2)}) async-start(bf16[8,1,1,24,512]{4,3,2,1,0:T(8,128)(2,1)} %bitcast_dynamic-update-slice_fusion), calls=%async_computation | async-start | bytes 393216 | tf_op jit(solution)/shard_map/all_to_all | solution.py:71
  25.3 5.9 %all-to-all-done = bf16[8,1,1,24,512]{4,3,2,1,0:T(8,128)(2,1)S(1)} async-done(((bf16[8,1,1,24,512]{4,3,2,1,0:T(8,128)(2,1)}), bf16[8,1,1,24,512]{4,3,2,1,0:T(8,128)(2,1)S(1)}, u32[]{:S(2)}, u32[]{:S(2)}) %all-to-all-start) | async-done | bytes 196640 | tf_op jit(solution)/shard_map/all_to_all | solution.py:71
  31.5 0.7 convolution_multiply_fusion.2
  32.3 1.2 fusion.111
  34.0 2.0 fusion.87
  36.0 2.9 %fusion.31 = bf16[128,4096]{0,1:T(8,128)(2,1)} fusion(f32[64,128,64]{1,2,0:T(8,128)} %fusion.87, bf16[1,1,128,4096]{2,3,1,0:T(8,128)(2,1)S(1)} %copy.41), kind=kLoop, calls=%fused_computation.37 | loop fusion | flops 1572864 | bytes 4194304 | tf_op jit(solution)/shard_map/convert_element_type | solution.py:35
  38.9 1.3 copy.50
  40.2 2.6 %collective-permute-start.2 = (bf16[128,4096]{0,1:T(8,128)(2,1)}, bf16[128,4096]{0,1:T(8,128)(2,1)}, u32[]{:S(2)}, u32[]{:S(2)}) collective-permute-start(bf16[128,4096]{0,1:T(8,128)(2,1)} %bitcast.143), channel_id=1, source_target_pairs={{0,28},{4,0},{8,4},{12,8},{16,12},{20,16},{24,20},{28,24},{1,29},{... | collective-permute-start | bytes 3145736 | tf_op jit(solution)/shard_map/ppermute | solution.py:12
  42.8 21.3 %collective-permute-done = bf16[128,4096]{0,1:T(8,128)(2,1)S(1)} collective-permute-done((bf16[128,4096]{0,1:T(8,128)(2,1)}, bf16[128,4096]{0,1:T(8,128)(2,1)S(1)}, u32[]{:S(2)}, u32[]{:S(2)}) %collective-permute-start) | collective-permute-done | bytes 1048608 | tf_op jit(solution)/shard_map/ppermute | solution.py:12
  64.7 0.7 fusion.22
  66.0 0.9 copy-done.11
  66.9 1.7 fusion.112
  68.5 3.3 %fusion.85 = f32[64,128,64]{1,2,0:T(8,128)} fusion(bf16[24,64,64]{2,1,0:T(8,128)(2,1)S(1)} %reshape_squeeze.2, f32[64,128]{1,0:T(8,128)} %get-tuple-element.15, f32[64,24,128]{2,1,0:T(8,128)} %copy-done.11), kind=kOutput, calls=%fused_computation.105 | convolution fusion | flops 25763864 | bytes 3112960 | tf_op jit(solution)/shard_map/hst,shd->thd/dot_general | solution.py:16
  71.9 1.8 fusion.30
  73.8 2.6 %fusion.83 = f32[64,24,128]{2,1,0:T(8,128)} fusion(bf16[128,64,64]{0,2,1:T(8,128)(2,1)} %bitcast.22, bf16[24,64,64]{2,1,0:T(8,128)(2,1)S(1)} %reshape_squeeze.2), kind=kOutput, calls=%fused_computation.103 | convolution fusion | flops 25165824 | bytes 2031616 | tf_op jit(solution)/shard_map/shd,thd->hst/dot_general | solution.py:16
  76.4 12.5 %collective-permute-done.1 = bf16[128,4096]{0,1:T(8,128)(2,1)S(1)} collective-permute-done((bf16[128,4096]{0,1:T(8,128)(2,1)S(1)}, bf16[128,4096]{0,1:T(8,128)(2,1)S(1)}, u32[]{:S(2)}, u32[]{:S(2)}) %collective-permute-start.1) | collective-permute-done | bytes 1048608 | tf_op jit(solution)/shard_map/ppermute | solution.py:12
  89.4 0.7 fusion.14
  90.2 1.0 copy-done.2
  91.7 0.9 copy-done.10
  92.6 1.7 fusion.113
  94.3 4.1 %fusion.58 = f32[64,64,128]{2,1,0:T(8,128)} fusion(f32[64,24,128]{2,1,0:T(8,128)} %fusion.83, bf16[24,64,64]{2,1,0:T(8,128)(2,1)} %copy-done.6, f32[64,24,128]{2,1,0:T(8,128)} %get-tuple-element.18, f32[64,128]{1,0:T(8,128)} %get-tuple-element.17), kind=kOutput, calls=%fused_computation.78 | convolution fusion | flops 26550296 | bytes 3899392 | tf_op jit(solution)/shard_map/hst,shd->thd/dot_general | solution.py:16
  98.3 3.3 %fusion.20 = (f32[4096]{0:T(1024)}, f32[128]{0:T(128)S(1)}) fusion(bf16[128,4096]{0,1:T(8,128)(2,1)S(1)} %collective-permute-done.1, f32[64,64,128]{2,1,0:T(8,128)} %fusion.58, f32[128]{0:T(128)} %copy-done.25, f32[4096]{0:T(1024)S(1)} %bitcast.146), kind=kLoop, calls=%fused_computation.25 | loop fusion | flops 3665792 | bytes 3179520 | tf_op jit(solution)/shard_map/reduce_sum | solution.py:56
  101.6 1.9 fusion.19
  103.8 12.3 %collective-permute-done.3 = bf16[128,4096]{0,1:T(8,128)(2,1)S(1)} collective-permute-done((bf16[128,4096]{0,1:T(8,128)(2,1)S(1)}, bf16[128,4096]{0,1:T(8,128)(2,1)S(1)}, u32[]{:S(2)}, u32[]{:S(2)}) %collective-permute-start.3) | collective-permute-done | bytes 1048608 | tf_op jit(solution)/shard_map/ppermute | solution.py:12
  116.1 1.3 convolution_bitcast_fusion.4
  117.4 4.1 %fusion.63 = f32[64,64,128]{2,1,0:T(8,128)} fusion(f32[64,24,128]{2,1,0:T(8,128)} %convolution_bitcast_fusion.4, bf16[24,64,64]{2,1,0:T(8,128)(2,1)} %copy-done.6, f32[64,24,128]{2,1,0:T(8,128)} %get-tuple-element.16, f32[64,128]{1,0:T(8,128)} %get-tuple-element.15), kind=kOutput, calls=%fused_computation.82 | convolution fusion | flops 26550296 | bytes 3899392 | tf_op jit(solution)/shard_map/hst,shd->thd/dot_general | solution.py:16
  121.5 3.3 %fusion.28 = (f32[4096]{0:T(1024)}, f32[128]{0:T(128)S(1)}) fusion(bf16[128,4096]{0,1:T(8,128)(2,1)S(1)} %collective-permute-done, f32[64,64,128]{2,1,0:T(8,128)} %fusion.63, f32[128]{0:T(128)} %copy-done.23, f32[4096]{0:T(1024)S(1)} %bitcast.148), kind=kLoop, calls=%fused_computation.33 | loop fusion | flops 3665792 | bytes 3179520 | tf_op jit(solution)/shard_map/reduce_sum | solution.py:56
  124.7 1.8 fusion.27
  126.5 2.8 %collective-permute-start.4 = (bf16[128,4096]{0,1:T(8,128)(2,1)}, bf16[128,4096]{0,1:T(8,128)(2,1)}, u32[]{:S(2)}, u32[]{:S(2)}) collective-permute-start(bf16[128,4096]{0,1:T(8,128)(2,1)} %fusion.27), channel_id=1, source_target_pairs={{0,28},{4,0},{8,4},{12,8},{16,12},{20,16},{24,20},{28,24},{1,29},{... | collective-permute-start | bytes 3145736 | tf_op jit(solution)/shard_map/ppermute | solution.py:12
  129.3 3.0 %convolution_bitcast_fusion.1 = f32[24,64,64]{2,0,1:T(8,128)} fusion(bf16[128,64,64]{0,2,1:T(8,128)(2,1)S(1)} %bitcast.142, f32[64,128]{1,0:T(8,128)} %get-tuple-element.15, f32[64,24,128]{2,1,0:T(8,128)} %copy-done.11), kind=kOutput, calls=%fused_computation.52 | convolution fusion | flops 25763864 | bytes 2260992 | tf_op jit(solution)/shard_map/hst,thd->shd/dot_general | solution.py:16
  132.3 3.4 %fusion.64 = f32[64,64,24]{1,2,0:T(8,128)} fusion(bf16[128,64,64]{0,2,1:T(8,128)(2,1)S(1)} %bitcast.140, f32[64,24,128]{2,1,0:T(8,128)} %convolution_bitcast_fusion.4, f32[64,24,128]{2,1,0:T(8,128)} %get-tuple-element.16, f32[64,128]{1,0:T(8,128)} %get-tuple-element.15), kind=kOutput, calls=%fused_computation.83 | convolution fusion | flops 26550296 | bytes 3047424 | tf_op jit(solution)/shard_map/hst,thd->shd/dot_general | solution.py:16
  135.7 6.2 %collective-permute-done.4 = bf16[128,4096]{0,1:T(8,128)(2,1)} collective-permute-done((bf16[128,4096]{0,1:T(8,128)(2,1)}, bf16[128,4096]{0,1:T(8,128)(2,1)}, u32[]{:S(2)}, u32[]{:S(2)}) %collective-permute-start.4) | collective-permute-done | bytes 1048608 | tf_op jit(solution)/shard_map/ppermute | solution.py:12
  142.0 3.2 %convolution_bitcast_fusion = f32[24,64,64]{2,0,1:T(8,128)} fusion(bf16[128,64,64]{0,2,1:T(8,128)(2,1)} %bitcast.29, f32[64,128]{1,0:T(8,128)S(1)} %copy-done.19, f32[64,24,128]{2,1,0:T(8,128)} %copy-done.15), kind=kOutput, calls=%fused_computation.51 | convolution fusion | flops 25763864 | bytes 2260992 | tf_op jit(solution)/shard_map/hst,thd->shd/dot_general | solution.py:16
  145.2 1.7 convolution_bitcast_fusion.3
  147.0 1.2 fusion.32
  148.3 1.7 fusion.69
  150.0 2.9 %fusion.56 = bf16[24,64,64]{2,0,1:T(8,128)(2,1)S(1)} fusion(f32[24,64,64]{2,0,1:T(8,128)} %convolution_bitcast_fusion, f32[24,64,64]{2,0,1:T(8,128)} %convolution_bitcast_fusion.1, bf16[128,64,64]{0,2,1:T(8,128)(2,1)} %bitcast.22, f32[64,128]{1,0:T(8,128)S(1)} %copy-done.20, f32[64,24,128]{2,1,0:T(8,128)} %copy-done.10), kind=kOutput, calls=%fused_computation.76 | convolution fusion | flops 26058776 | bytes 2850816 | tf_op jit(solution)/shard_map/hst,thd->shd/dot_general | solution.py:16
  153.4 3.0 %copy.60 = bf16[1,1,24,4096]{2,1,0,3:T(2,128)(2,1)S(1)} copy(bf16[1,1,24,4096]{3,2,1,0:T(8,128)(2,1)S(1)} %convert_element_type.128) | data formatting | bytes 393216 | tf_op jit(solution)/shard_map/convert_element_type | solution.py:111
  156.9 23.5 %reduce.6 = bf16[4096,24]{1,0:T(8,128)(2,1)} reduce(bf16[4096,1,1,24]{3,2,1,0:T(2,128)(2,1)S(1)} %bitcast.133, bf16[]{:T(256)} %broadcast.115), dimensions={1,2}, to_apply=%bitcast.110.reduce_sub_computation | reduce | bytes 393218
  180.4 3.4 %reshape.202 = bf16[8,2,6144]{2,1,0:T(2,128)(2,1)} reshape(bf16[4096,24]{1,0:T(8,128)(2,1)} %reduce.6) | data formatting | bytes 393216
  183.7 4.1 %all-to-all-start.3 = ((bf16[8,2,6144]{2,1,0:T(2,128)(2,1)}), bf16[8,2,6144]{2,1,0:T(2,128)(2,1)S(1)}, u32[]{:S(2)}, u32[]{:S(2)}) async-start(bf16[8,2,6144]{2,1,0:T(2,128)(2,1)} %reshape.202), calls=%async_computation.3 | async-start | bytes 393216 | tf_op jit(solution)/shard_map/all_to_all | solution.py:110
  187.8 3.0 %fusion.57 = bf16[24,64,64]{2,0,1:T(8,128)(2,1)S(1)} fusion(f32[64,64,24]{1,2,0:T(8,128)} %fusion.69, f32[64,64,24]{1,2,0:T(8,128)} %fusion.64, bf16[128,64,64]{0,2,1:T(8,128)(2,1)S(1)} %bitcast.138, f32[64,24,128]{2,1,0:T(8,128)} %fusion.83, f32[64,24,128]{2,1,0:T(8,128)} %get-tuple-element.18, f32[64,128]{1,0:T(8,128)S(1)} %copy-done.20), kind=kOutput, calls=%fused_computation.77 | convolution fusion | flops 26845208 | bytes 3637248 | tf_op jit(solution)/shard_map/hst,thd->shd/dot_general | solution.py:16
  191.2 2.8 %copy.57 = bf16[1,1,24,4096]{2,1,0,3:T(2,128)(2,1)S(1)} copy(bf16[1,1,24,4096]{3,2,1,0:T(8,128)(2,1)S(1)} %convert_element_type.125) | data formatting | bytes 393216 | tf_op jit(solution)/shard_map/convert_element_type | solution.py:104
  194.0 22.4 %reduce.5 = bf16[4096,24]{1,0:T(8,128)(2,1)S(1)} reduce(bf16[4096,1,1,24]{3,2,1,0:T(2,128)(2,1)S(1)} %bitcast.134, bf16[]{:T(256)} %broadcast.115), dimensions={1,2}, to_apply=%bitcast.108.reduce_sub_computation | reduce | bytes 393218
  216.5 2.0 reshape.200
  218.5 4.2 %all-to-all-start.2 = ((bf16[8,2,6144]{2,1,0:T(2,128)(2,1)}), bf16[8,2,6144]{2,1,0:T(2,128)(2,1)S(1)}, u32[]{:S(2)}, u32[]{:S(2)}) async-start(bf16[8,2,6144]{2,1,0:T(2,128)(2,1)} %reshape.200), calls=%async_computation.2 | async-start | bytes 393216 | tf_op jit(solution)/shard_map/all_to_all | solution.py:103
  222.7 19.6 %psum.7 = f32[1,4096]{1,0:T(1,128)} all-reduce(f32[1,4096]{1,0:T(1,128)S(1)} %bitcast.157), channel_id=1, replica_groups=mesh['section'=8,'dp'=4] {'dp'}, use_global_device_ids=true, to_apply=%region_17.0 | all-reduce | flops 4096 | bytes 32768 | tf_op jit(solution)/shard_map/psum | solution.py:118
  242.3 3.0 %reshape.203 = bf16[4096,1,1,24]{3,2,1,0:T(2,128)(2,1)S(1)} reshape(bf16[8,2,6144]{2,1,0:T(2,128)(2,1)S(1)} %all-to-all-done.3) | data formatting | bytes 393216
  245.2 2.1 copy.61
  247.4 0.7 copy.64
  248.2 3.0 %reshape.201 = bf16[4096,1,1,24]{3,2,1,0:T(2,128)(2,1)S(1)} reshape(bf16[8,2,6144]{2,1,0:T(2,128)(2,1)S(1)} %all-to-all-done.2) | data formatting | bytes 393216
  251.1 2.1 copy.58
  253.3 0.7 copy.63
  (87 shorter events, 6.5 us)
Async XLA Ops:
  0.6 20.2 %all-to-all-start.1 = ((bf16[1,8,24,512]{3,2,0,1:T(8,128)(2,1)}), bf16[1,8,24,512]{3,2,0,1:T(8,128)(2,1)S(1)}, u32[]{:S(2)}, u32[]{:S(2)}) async-start(bf16[1,8,24,512]{3,2,0,1:T(8,128)(2,1)} %bitcast.156), calls=%async_computation.1 | async-start | bytes 393216 | tf_op jit(solution)/shard_map/all_to_all | solution.py:76
  7.8 23.7 %copy-start.21 = (f32[64,64]{1,0:T(8,128)}, f32[64,64]{1,0:T(8,128)S(1)}, u32[]{:S(2)}) copy-start(f32[64,64]{1,0:T(8,128)S(1)} %mul.89) | copy-start | bytes 49156
  20.8 10.4 %all-to-all-start = ((bf16[8,1,1,24,512]{4,3,2,1,0:T(8,128)(2,1)}), bf16[8,1,1,24,512]{4,3,2,1,0:T(8,128)(2,1)S(1)}, u32[]{:S(2)}, u32[]{:S(2)}) async-start(bf16[8,1,1,24,512]{4,3,2,1,0:T(8,128)(2,1)} %bitcast_dynamic-update-slice_fusion), calls=%async_computation | async-start | bytes 393216 | tf_op jit(solution)/shard_map/all_to_all | solution.py:71
  25.0 7.2 %copy-start.27 = (f32[128]{0:T(128)}, f32[128]{0:T(128)S(1)}, u32[]{:S(2)}) copy-start(f32[128]{0:T(128)S(1)} %add_rsqrt_fusion.2) | copy-start | bytes 1540
  31.5 4.5 %copy-start.6 = (bf16[24,64,64]{2,1,0:T(8,128)(2,1)}, bf16[24,64,64]{2,1,0:T(8,128)(2,1)S(1)}, u32[]{:S(2)}) copy-start(bf16[24,64,64]{2,1,0:T(8,128)(2,1)S(1)} %reshape_squeeze_reshape.2) | copy-start | bytes 589828
  32.3 1.2 copy-start.15
  33.4 0.6 copy-start.18
  36.0 2.9 %copy-start.12 = (bf16[1,1,128,4096]{3,2,1,0:T(8,128)(2,1)S(1)}, bf16[1,1,128,4096]{3,2,1,0:T(8,128)(2,1)}, u32[]{:S(2)}) copy-start(bf16[1,1,128,4096]{3,2,1,0:T(8,128)(2,1)} %param.9) | copy-start | bytes 3145732
  38.9 25.9 %copy-start.13 = (f32[1,4096]{1,0:T(1,128)S(1)}, f32[1,4096]{1,0:T(1,128)}, u32[]{:S(2)}) copy-start(f32[1,4096]{1,0:T(1,128)} %param.8) | copy-start | bytes 49156
  38.9 25.3 %collective-permute-start = (bf16[128,4096]{0,1:T(8,128)(2,1)}, bf16[128,4096]{0,1:T(8,128)(2,1)S(1)}, u32[]{:S(2)}, u32[]{:S(2)}) collective-permute-start(bf16[128,4096]{0,1:T(8,128)(2,1)} %fusion.31), channel_id=1, source_target_pairs={{0,4},{4,8},{8,12},{12,16},{16,20},{20,24},{24,28},{28,0},{1,5},{5... | collective-permute-start | bytes 3145736 | tf_op jit(solution)/shard_map/ppermute | solution.py:12
  40.2 25.3 %copy-start.7 = (bf16[24,64,64]{2,1,0:T(8,128)(2,1)S(1)}, bf16[24,64,64]{2,1,0:T(8,128)(2,1)}, u32[]{:S(2)}) copy-start(bf16[24,64,64]{2,1,0:T(8,128)(2,1)} %copy-done.6) | copy-start | bytes 589828
  40.2 33.6 %collective-permute-start.2 = (bf16[128,4096]{0,1:T(8,128)(2,1)}, bf16[128,4096]{0,1:T(8,128)(2,1)}, u32[]{:S(2)}, u32[]{:S(2)}) collective-permute-start(bf16[128,4096]{0,1:T(8,128)(2,1)} %bitcast.143), channel_id=1, source_target_pairs={{0,28},{4,0},{8,4},{12,8},{16,12},{20,16},{24,20},{28,24},{1,29},{... | collective-permute-start | bytes 3145736 | tf_op jit(solution)/shard_map/ppermute | solution.py:12
  64.7 0.7 copy-start.23
  65.5 6.4 %copy-start.4 = (bf16[128,4096]{0,1:T(8,128)(2,1)}, bf16[128,4096]{0,1:T(8,128)(2,1)S(1)}, u32[]{:S(2)}) copy-start(bf16[128,4096]{0,1:T(8,128)(2,1)S(1)} %fusion.22) | copy-start | bytes 3145732
  66.0 0.9 copy-start.11
  73.7 15.2 %collective-permute-start.1 = (bf16[128,4096]{0,1:T(8,128)(2,1)S(1)}, bf16[128,4096]{0,1:T(8,128)(2,1)S(1)}, u32[]{:S(2)}, u32[]{:S(2)}) collective-permute-start(bf16[128,4096]{0,1:T(8,128)(2,1)S(1)} %fusion.30), channel_id=1, source_target_pairs={{0,4},{4,8},{8,12},{12,16},{16,20},{20,24},{24,28},{28,0},{1,5},{5... | collective-permute-start | bytes 3145736 | tf_op jit(solution)/shard_map/ppermute | solution.py:12
  76.4 14.8 %copy-start.8 = (bf16[24,64,64]{2,1,0:T(8,128)(2,1)S(1)}, bf16[24,64,64]{2,1,0:T(8,128)(2,1)}, u32[]{:S(2)}) copy-start(bf16[24,64,64]{2,1,0:T(8,128)(2,1)} %copy-done.6) | copy-start | bytes 589828
  89.4 0.7 copy-start.25
  90.2 1.0 copy-start.2
  91.6 0.9 copy-start.10
  98.3 3.3 %copy-start = (f32[64,64,128]{2,1,0:T(8,128)S(1)}, f32[64,64,128]{2,1,0:T(8,128)}, u32[]{:S(2)}) copy-start(f32[64,64,128]{2,1,0:T(8,128)} %fusion.58) | copy-start | bytes 6291460
  98.3 3.3 %copy-start.26 = (f32[128]{0:T(128)S(1)}, f32[128]{0:T(128)}, u32[]{:S(2)}) copy-start(f32[128]{0:T(128)} %copy-done.25) | copy-start | bytes 1540
  103.5 12.6 %collective-permute-start.3 = (bf16[128,4096]{0,1:T(8,128)(2,1)S(1)}, bf16[128,4096]{0,1:T(8,128)(2,1)S(1)}, u32[]{:S(2)}, u32[]{:S(2)}) collective-permute-start(bf16[128,4096]{0,1:T(8,128)(2,1)S(1)} %fusion.19), channel_id=1, source_target_pairs={{0,28},{4,0},{8,4},{12,8},{16,12},{20,16},{24,20},{28,24},{1,29},{... | collective-permute-start | bytes 3145736 | tf_op jit(solution)/shard_map/ppermute | solution.py:12
  121.5 3.3 %copy-start.1 = (f32[64,64,128]{2,1,0:T(8,128)S(1)}, f32[64,64,128]{2,1,0:T(8,128)}, u32[]{:S(2)}) copy-start(f32[64,64,128]{2,1,0:T(8,128)} %fusion.63) | copy-start | bytes 6291460
  121.5 3.3 %copy-start.24 = (f32[128]{0:T(128)S(1)}, f32[128]{0:T(128)}, u32[]{:S(2)}) copy-start(f32[128]{0:T(128)} %copy-done.23) | copy-start | bytes 1540
  126.5 5.8 %copy-start.5 = (bf16[128,4096]{0,1:T(8,128)(2,1)S(1)}, bf16[128,4096]{0,1:T(8,128)(2,1)}, u32[]{:S(2)}) copy-start(bf16[128,4096]{0,1:T(8,128)(2,1)} %copy-done.4) | copy-start | bytes 3145732
  126.5 15.4 %collective-permute-start.4 = (bf16[128,4096]{0,1:T(8,128)(2,1)}, bf16[128,4096]{0,1:T(8,128)(2,1)}, u32[]{:S(2)}, u32[]{:S(2)}) collective-permute-start(bf16[128,4096]{0,1:T(8,128)(2,1)} %fusion.27), channel_id=1, source_target_pairs={{0,28},{4,0},{8,4},{12,8},{16,12},{20,16},{24,20},{28,24},{1,29},{... | collective-permute-start | bytes 3145736 | tf_op jit(solution)/shard_map/ppermute | solution.py:12
  132.3 9.7 %copy-start.19 = (f32[64,128]{1,0:T(8,128)S(1)}, f32[64,128]{1,0:T(8,128)}, u32[]{:S(2)}) copy-start(f32[64,128]{1,0:T(8,128)} %copy-done.18) | copy-start | bytes 98308
  145.2 1.8 copy-start.9
  145.2 1.8 copy-start.14
  145.2 1.8 copy-start.28
  147.0 1.2 copy-start.22
  148.3 1.8 copy-start.20
  156.9 30.9 %copy-start.3 = (bf16[128,4096]{0,1:T(8,128)(2,1)S(1)}, bf16[128,4096]{0,1:T(8,128)(2,1)}, u32[]{:S(2)}) copy-start(bf16[128,4096]{0,1:T(8,128)(2,1)} %copy-done.2) | copy-start | bytes 3145732
  183.7 34.8 %all-to-all-start.3 = ((bf16[8,2,6144]{2,1,0:T(2,128)(2,1)}), bf16[8,2,6144]{2,1,0:T(2,128)(2,1)S(1)}, u32[]{:S(2)}, u32[]{:S(2)}) async-start(bf16[8,2,6144]{2,1,0:T(2,128)(2,1)} %reshape.202), calls=%async_computation.3 | async-start | bytes 393216 | tf_op jit(solution)/shard_map/all_to_all | solution.py:110
  194.0 28.7 %copy-start.16 = (f32[4096]{0:T(1024)S(1)}, f32[4096]{0:T(1024)}, u32[]{:S(2)}) copy-start(f32[4096]{0:T(1024)} %get-tuple-element.11) | copy-start | bytes 49156
  194.0 28.7 %copy-start.17 = (f32[4096]{0:T(1024)S(1)}, f32[4096]{0:T(1024)}, u32[]{:S(2)}) copy-start(f32[4096]{0:T(1024)} %get-tuple-element.9) | copy-start | bytes 49156
  218.5 29.7 %all-to-all-start.2 = ((bf16[8,2,6144]{2,1,0:T(2,128)(2,1)}), bf16[8,2,6144]{2,1,0:T(2,128)(2,1)S(1)}, u32[]{:S(2)}, u32[]{:S(2)}) async-start(bf16[8,2,6144]{2,1,0:T(2,128)(2,1)} %reshape.200), calls=%async_computation.2 | async-start | bytes 393216 | tf_op jit(solution)/shard_map/all_to_all | solution.py:103
